TPU v7x, 256 devices: a whole 4x4x8 slice. The times are simulated.
256 devices in a mesh: row: 8 (over z_hi, y), col: 32 (over x, z_lo, core).
Axes of the slice: x: 4, y: 4, z: 8 (z_hi: 2, z_lo: 4; z = z_hi * 4 + z_lo), core: 2. Of those that a mesh axis runs over, the one named last changes fastest.
Arguments:
- features: bfloat16 [65536, 256], P('col', 'row'), may hold values from -6 to 6
- block_values: bfloat16 [8, 32, 256, 128, 128], P('row', 'col'), may hold values from -0.046875 to 0.046875
- block_coords: int32 [8, 32, 2, 256], P('row', 'col'), may hold values from 0 to 63, as said below
- live_blocks: int32 [8, 32], P('row', 'col'), may hold values from 32 to 256, as said below
- weight: bfloat16 [256, 256], replicated, may hold values from -0.375 to 0.375
- bias: float32 [256], replicated, may hold values from -3 to 3
- cotangent: bfloat16 [65536, 256], P(('row', 'col')), may hold values from -6 to 6
Outputs:
- out: bfloat16 [65536, 256], P(('row', 'col'))
- grad_x: bfloat16 [65536, 256], P('col', 'row')
- grad_weight: float32 [256, 256], replicated
- grad_bias: float32 [256], replicated
Inputs may be any that keep to these rules, and one draw needn't show every extreme that they name: `block_coords`: within one tile the 256 slots name distinct pairs of a row block (0 to 63) and a column block (0 to 15). Only the first live_blocks[i, j] slots of tile (i, j) belong to the adjacency; some tile has all 256 slots live.
All inputs are finite; a program needn't handle non-finite values.
Results may differ from a plain program's by a relative error of at most 0.0075.
Values may be sent and summed in bfloat16 or wider, within the bound.
A program may use at most 128 MiB of HBM per device.

v0:
```python
import math
import jax
import jax.numpy as jnp
from jax import lax
from jax.sharding import PartitionSpec as P


def block_products(block_vals, source, dst_index, src_index, live_count, out_blocks, transposed):
    slot_total = block_vals.shape[0]
    block_size = block_vals.shape[1]
    feat_width = source.shape[2]
    group_size = math.gcd(slot_total, 64)
    pattern = "sab,saf->sbf" if transposed else "sab,sbf->saf"
    offsets = jnp.arange(group_size, dtype=jnp.int32)

    def one_group(turn, totals):
        first_slot = turn * group_size
        slab_vals = lax.dynamic_slice_in_dim(block_vals, first_slot, group_size, 0)
        take_from = lax.dynamic_slice_in_dim(src_index, first_slot, group_size, 0)
        put_to = lax.dynamic_slice_in_dim(dst_index, first_slot, group_size, 0)
        picked = jnp.take(source, take_from, axis=0)
        products = jnp.einsum(pattern, slab_vals, picked, preferred_element_type=jnp.float32)
        alive_mask = first_slot + offsets < live_count
        products = jnp.where(alive_mask[:, None, None], products, 0.0)
        return totals.at[put_to].add(products)

    start_totals = jnp.zeros((out_blocks, block_size, feat_width), jnp.float32)
    turns = slot_total // group_size
    return lax.fori_loop(0, turns, one_group, start_totals)


def on_device(features, block_values, block_coords, live_blocks, weight, bias, cotangent):
    block_vals = block_values[0, 0]
    row_ids = block_coords[0, 0, 0]
    col_ids = block_coords[0, 0, 1]
    live_count = live_blocks[0, 0]
    block_size = block_vals.shape[1]
    feat_width = weight.shape[0]
    col_count = lax.axis_size("col")
    feat_tile = lax.all_gather(features, "row", axis=1, tiled=True)
    col_blocks = feat_tile.shape[0] // block_size
    row_blocks = cotangent.shape[0] * col_count // block_size
    feat_blocks = feat_tile.reshape(col_blocks, block_size, feat_width)
    partial_value = block_products(
        block_vals, feat_blocks, row_ids, col_ids, live_count, row_blocks, False
    )
    partial_value = partial_value.reshape(row_blocks * block_size, feat_width)
    aggregate = lax.psum_scatter(partial_value, "col", scatter_dimension=0, tiled=True).astype(
        jnp.bfloat16
    )
    preact = jnp.dot(aggregate, weight, preferred_element_type=jnp.float32) + bias
    sigmoid_v = jax.nn.sigmoid(preact)
    out = (preact * sigmoid_v).astype(jnp.bfloat16)
    derivative = sigmoid_v * (1.0 + preact * (1.0 - sigmoid_v))
    grad_pre = (cotangent.astype(jnp.float32) * derivative).astype(jnp.bfloat16)
    weight_term = lax.dot_general(
        aggregate, grad_pre, (((0,), (0,)), ((), ())), preferred_element_type=jnp.float32
    )
    bias_term = jnp.sum(grad_pre.astype(jnp.float32), axis=0)
    weight_sum, bias_sum = lax.psum((weight_term, bias_term), ("row", "col"))
    norm_factor = (feat_tile.shape[0] * col_count) ** (-0.5)
    grad_weight = weight_sum * norm_factor
    grad_bias = bias_sum * norm_factor
    grad_agg = lax.dot_general(
        grad_pre, weight, (((1,), (1,)), ((), ())), preferred_element_type=jnp.float32
    ).astype(jnp.bfloat16)
    grad_tile = lax.all_gather(grad_agg, "col", axis=0, tiled=True)
    grad_blocks = grad_tile.reshape(row_blocks, block_size, feat_width)
    partial_x = block_products(
        block_vals, grad_blocks, col_ids, row_ids, live_count, col_blocks, True
    )
    partial_x = partial_x.reshape(col_blocks * block_size, feat_width)
    grad_x = lax.psum_scatter(partial_x, "row", scatter_dimension=1, tiled=True).astype(
        jnp.bfloat16
    )
    return (out, grad_x, grad_weight, grad_bias)


def solution(mesh):
    in_specs = (
        P("col", "row"),
        P("row", "col", None, None, None),
        P("row", "col", None, None),
        P("row", "col"),
        P(),
        P(),
        P(("row", "col"), None),
    )
    out_specs = (P(("row", "col"), None), P("col", "row"), P(), P())
    return jax.shard_map(
        on_device, mesh=mesh, in_specs=in_specs, out_specs=out_specs, check_vma=False
    )
```

profile of v0, /device:TPU:2, one launch (start us, length us, event | category | flops | bytes accessed | tf_op | source)
XLA Modules:
  0.0 785.1 jit_solution(2173765968436024874)
XLA Ops:
  8.7 66.8 %all-gather.3.cloned.1.call-done = bf16[2048,256]{0,1:T(8,128)(2,1)} async-done(((bf16[2048,32]{0,1:T(8,128)(2,1)}), bf16[2048,256]{0,1:T(8,128)(2,1)}) %all-gather.3.cloned.1.call-update) | async-done | bytes 1048592 | tf_op jit(solution)/shard_map/all_gather | solution.py:40
  81.3 122.0 %while.28 = (s32[]{:T(128)}, f32[64,128,256]{2,1,0:T(8,128)}, s32[256]{0:T(256)S(1)}, s32[]{:T(128)}, bf16[256,128,128]{2,1,0:T(8,128)(2,1)}, /*index=5*/s32[256...) while((s32[]{:T(128)}, f32[64,128,256]{2,1,0:T(8,128)}, ...), condition=%wide.region_2.3_spmd.clone, body=%wide.region_0.2_spmd.clone.sunk | while | flops 543164096 | bytes 48240816 | solution.py:29
  84.8 7.4 broadcast_select_fusion.4
  92.2 19.6 %scatter_fusion = f32[64,128,256]{2,1,0:T(8,128)} fusion(f32[64,128,256]{2,1,0:T(8,128)} %get-tuple-element.472, s32[64]{0:T(128)S(1)} %compare_select_fusion.8, f32[64,128,256]{2,1,0:T(8,128)} %broadcast_select_fusion.4), kind=kCustom, calls=%fused_computation.2.clone.clone.1 | custom fusion | flops 2097152 | bytes 25166080 | tf_op jit(solution)/shard_map/while/body/eval_jaxpr/scatter-add | solution.py:25
  122.8 19.4 %scatter_fusion = f32[64,128,256]{2,1,0:T(8,128)} fusion(f32[64,128,256]{2,1,0:T(8,128)} %get-tuple-element.472, s32[64]{0:T(128)S(1)} %compare_select_fusion.8, f32[64,128,256]{2,1,0:T(8,128)} %broadcast_select_fusion.4), kind=kCustom, calls=%fused_computation.2.clone.clone.1 | custom fusion | flops 2097152 | bytes 25166080 | tf_op jit(solution)/shard_map/while/body/eval_jaxpr/scatter-add | solution.py:25
  145.7 7.4 broadcast_select_fusion.4
  153.1 19.6 %scatter_fusion = f32[64,128,256]{2,1,0:T(8,128)} fusion(f32[64,128,256]{2,1,0:T(8,128)} %get-tuple-element.472, s32[64]{0:T(128)S(1)} %compare_select_fusion.8, f32[64,128,256]{2,1,0:T(8,128)} %broadcast_select_fusion.4), kind=kCustom, calls=%fused_computation.2.clone.clone.1 | custom fusion | flops 2097152 | bytes 25166080 | tf_op jit(solution)/shard_map/while/body/eval_jaxpr/scatter-add | solution.py:25
  176.2 7.4 broadcast_select_fusion.4
  183.6 19.6 %scatter_fusion = f32[64,128,256]{2,1,0:T(8,128)} fusion(f32[64,128,256]{2,1,0:T(8,128)} %get-tuple-element.472, s32[64]{0:T(128)S(1)} %compare_select_fusion.8, f32[64,128,256]{2,1,0:T(8,128)} %broadcast_select_fusion.4), kind=kCustom, calls=%fused_computation.2.clone.clone.1 | custom fusion | flops 2097152 | bytes 25166080 | tf_op jit(solution)/shard_map/while/body/eval_jaxpr/scatter-add | solution.py:25
  203.3 138.4 %reduce-scatter.3.cloned.1.call-done = f32[256,256]{1,0:T(8,128)} async-done(((f32[8192,256]{1,0:T(8,128)}), f32[256,256]{1,0:T(8,128)}) %reduce-scatter.3.cloned.1.call-update) | async-done | bytes 262160 | tf_op jit(solution)/shard_map/reduce_scatter | solution.py:48
  344.6 12.0 %copy.11 = bf16[1,1,256,128,128]{3,4,2,1,0:T(8,128)(2,1)} copy(bf16[1,1,256,128,128]{4,3,2,1,0:T(8,128)(2,1)} %bitcast.18) | data formatting | bytes 16777216 | tf_op args[1]
  357.6 65.8 %all-gather.5.cloned.1.call-done = bf16[8192,256]{1,0:T(8,128)(2,1)} async-done(((bf16[256,256]{1,0:T(8,128)(2,1)}), bf16[8192,256]{1,0:T(8,128)(2,1)}) %all-gather.5.cloned.1.call-update) | async-done | bytes 4194320 | tf_op jit(solution)/shard_map/all_gather | solution.py:67
  423.6 102.6 %while.29 = (s32[]{:T(128)}, f32[16,128,256]{2,1,0:T(8,128)S(1)}, s32[256]{0:T(256)S(1)}, s32[]{:T(128)}, bf16[256,128,128]{1,2,0:T(8,128)(2,1)}, /*index=5*/s32...) while((s32[]{:T(128)}, f32[16,128,256]{2,1,0:T(8,128)S(1)}, ...), condition=%wide.region_6.7_spmd.clone, body=%wide.region_4.6_spmd.clone.sunk | while | flops 543164096 | bytes 48240816 | solution.py:29
  429.4 7.4 broadcast_select_fusion.5
  436.8 12.4 %scatter_fusion.1 = f32[16,128,256]{2,1,0:T(8,128)S(1)} fusion(f32[16,128,256]{2,1,0:T(8,128)S(1)} %get-tuple-element.505, s32[64]{0:T(128)S(1)} %compare_select_fusion.9, f32[64,128,256]{2,1,0:T(8,128)} %broadcast_select_fusion.5), kind=kCustom, calls=%fused_computation.3.clone.clone.1 | custom fusion | flops 2097152 | bytes 25166080 | tf_op jit(solution)/shard_map/while/body/eval_jaxpr/scatter-add | solution.py:25
  455.0 7.4 broadcast_select_fusion.5
  462.5 12.5 %scatter_fusion.1 = f32[16,128,256]{2,1,0:T(8,128)S(1)} fusion(f32[16,128,256]{2,1,0:T(8,128)S(1)} %get-tuple-element.505, s32[64]{0:T(128)S(1)} %compare_select_fusion.9, f32[64,128,256]{2,1,0:T(8,128)} %broadcast_select_fusion.5), kind=kCustom, calls=%fused_computation.3.clone.clone.1 | custom fusion | flops 2097152 | bytes 25166080 | tf_op jit(solution)/shard_map/while/body/eval_jaxpr/scatter-add | solution.py:25
  480.7 7.4 broadcast_select_fusion.5
  488.2 12.4 %scatter_fusion.1 = f32[16,128,256]{2,1,0:T(8,128)S(1)} fusion(f32[16,128,256]{2,1,0:T(8,128)S(1)} %get-tuple-element.505, s32[64]{0:T(128)S(1)} %compare_select_fusion.9, f32[64,128,256]{2,1,0:T(8,128)} %broadcast_select_fusion.5), kind=kCustom, calls=%fused_computation.3.clone.clone.1 | custom fusion | flops 2097152 | bytes 25166080 | tf_op jit(solution)/shard_map/while/body/eval_jaxpr/scatter-add | solution.py:25
  506.3 7.4 broadcast_select_fusion.5
  513.8 12.4 %scatter_fusion.1 = f32[16,128,256]{2,1,0:T(8,128)S(1)} fusion(f32[16,128,256]{2,1,0:T(8,128)S(1)} %get-tuple-element.505, s32[64]{0:T(128)S(1)} %compare_select_fusion.9, f32[64,128,256]{2,1,0:T(8,128)} %broadcast_select_fusion.5), kind=kCustom, calls=%fused_computation.3.clone.clone.1 | custom fusion | flops 2097152 | bytes 25166080 | tf_op jit(solution)/shard_map/while/body/eval_jaxpr/scatter-add | solution.py:25
  528.1 76.1 %psum.15 = f32[256]{0:T(256)S(1)} all-reduce(f32[256]{0:T(256)S(1)} %get-tuple-element.355), channel_id=1, replica_groups=mesh['row'=8,'col'=32] {'row','col'}, use_global_device_ids=true, to_apply=%region_10.11 | all-reduce | flops 256 | bytes 2048 | tf_op jit(solution)/shard_map/psum | solution.py:60
  604.8 74.2 %all-reduce.2.cloned.1.call-done = f32[256,256]{1,0:T(8,128)} async-done(((f32[256,256]{1,0:T(8,128)}), f32[256,256]{1,0:T(8,128)}) %all-reduce.2.cloned.1.call-update) | async-done | bytes 262160 | tf_op jit(solution)/shard_map/psum | solution.py:60
  680.7 96.3 %reduce-scatter.5.cloned.1.call-done = f32[2048,32]{0,1:T(8,128)} async-done(((f32[2048,256]{0,1:T(8,128)}), f32[2048,32]{0,1:T(8,128)}) %reduce-scatter.5.cloned.1.call-update) | async-done | bytes 262160 | tf_op jit(solution)/shard_map/reduce_scatter | solution.py:73
  (62 shorter events, 61.8 us)
Async XLA Ops:
  7.2 334.6 %copy-start = (bf16[256,256]{1,0:T(8,128)(2,1)S(1)}, bf16[256,256]{1,0:T(8,128)(2,1)}, u32[]{:S(2)}) copy-start(bf16[256,256]{1,0:T(8,128)(2,1)} %param.15) | copy-start | bytes 393220
  7.2 68.4 %all-gather.3.cloned.1.call-start = ((), (), s32[]{:S(2)}) async-start(), calls=%async_computation.2 | async-start | bytes 1179648 | tf_op jit(solution)/shard_map/all_gather | solution.py:40
  7.9 333.8 %reduce-scatter.3.cloned.1.call-start = ((), (), s32[]{:S(2)}) async-start(), calls=%async_computation.3 | async-start | bytes 8650752 | tf_op jit(solution)/shard_map/reduce_scatter | solution.py:48
  203.3 138.5 %copy-start.2 = (bf16[256,256]{1,0:T(8,128)(2,1)S(1)}, bf16[256,256]{1,0:T(8,128)(2,1)}, u32[]{:S(2)}) copy-start(bf16[256,256]{1,0:T(8,128)(2,1)} %param.17) | copy-start | bytes 393220
  203.3 138.5 %copy-start.3 = (f32[256]{0:T(256)S(1)}, f32[256]{0:T(256)}, u32[]{:S(2)}) copy-start(f32[256]{0:T(256)} %param.16) | copy-start | bytes 3076
  203.3 220.1 %all-gather.5.cloned.1.call-start = ((), (), s32[]{:S(2)}) async-start(), calls=%async_computation.4 | async-start | bytes 4325376 | tf_op jit(solution)/shard_map/all_gather | solution.py:67
  344.5 12.1 %copy-start.1 = (f32[256,256]{1,0:T(8,128)S(1)}, f32[256,256]{1,0:T(8,128)}, u32[]{:S(2)}) copy-start(f32[256,256]{1,0:T(8,128)} %reduce-scatter.3.cloned.1.call-done) | copy-start | bytes 786436
  344.5 334.4 %all-reduce.2.cloned.1.call-start = ((), (), s32[]{:S(2)}) async-start(), calls=%async_computation.6 | async-start | bytes 524288 | tf_op jit(solution)/shard_map/psum | solution.py:60
  357.5 419.4 %reduce-scatter.5.cloned.1.call-start = ((), (), s32[]{:S(2)}) async-start(), calls=%async_computation.5 | async-start | bytes 2359296 | tf_op jit(solution)/shard_map/reduce_scatter | solution.py:73
Sparse Core Ops, SparseCore 0:
  10.6 64.8 all-gather.2
  203.4 138.2 reduce-scatter.2
  344.7 78.7 all-gather.4
  429.3 249.6 all-reduce.1
  682.9 93.9 reduce-scatter.4
where the time goes:
time: 787 us; the launch traced here: 785 us
  waiting for transfers between devices  442 us (56%)
  other arithmetic  138 us (18%)
  blocking collectives  76.1 us (10%)
  matrix products  62.7 us (8%)
  local copies, waits for them, and re-layouts  51.5 us (7%)
  between operations  13.8 us (2%)
    reduce_scatter x1, waiting for transfers between devices, on_device(): lax.psum_scatter(partial_value, 'col', scatter_dimension=0, tiled=True)  138 us
    scatter-add x8, other arithmetic, one_group(): return totals.at[put_to].add(products)  128 us
    reduce_scatter x1, waiting for transfers between devices, on_device(): lax.psum_scatter(partial_x, 'row', scatter_dimension=1, tiled=True)  96.3 us
    psum x1, blocking collectives, on_device(): weight_sum, bias_sum = lax.psum((weight_term, bias_term), ('row', 'col'))  76.1 us
    psum x1, waiting for transfers between devices, on_device(): weight_sum, bias_sum = lax.psum((weight_term, bias_term), ('row', 'col'))  74.2 us
    all_gather x1, waiting for transfers between devices, on_device(): feat_tile = lax.all_gather(features, 'row', axis=1, tiled=True)  66.8 us
    all_gather x1, waiting for transfers between devices, on_device(): grad_tile = lax.all_gather(grad_agg, 'col', axis=0, tiled=True)  65.8 us
    dot_general x8, matrix products, one_group(): jnp.einsum(pattern, slab_vals, picked, preferred_element_type=jnp.float32)  59 us
  transfers between devices with their start and end apart: 5, of which 5 were waited for; matrix products, arithmetic and copies ran while one was open for 15% of the time, Pallas kernels for 0%

commit v1 on v0

--- a/solution.py
+++ b/solution.py
@@ -57,7 +57,7 @@
         aggregate, grad_pre, (((0,), (0,)), ((), ())), preferred_element_type=jnp.float32
     )
     bias_term = jnp.sum(grad_pre.astype(jnp.float32), axis=0)
-    weight_sum, bias_sum = lax.psum((weight_term, bias_term), ("row", "col"))
+    weight_sum, bias_sum = lax.psum(lax.psum((weight_term, bias_term), "row"), "col")
     norm_factor = (feat_tile.shape[0] * col_count) ** (-0.5)
     grad_weight = weight_sum * norm_factor
     grad_bias = bias_sum * norm_factor

time: 787 us -> 913 us (1.16)
  waiting for transfers between devices: 442 us -> 556 us
  blocking collectives: 76.1 us -> 87.6 us
    psum x1 -> x2, waiting for transfers between devices: 74.2 us -> 180 us  [the longest x1 110 us: on_device(): lax.psum((weight_term, bias_term), 'row')]
    reduce_scatter x1, waiting for transfers between devices: 96.3 us -> 109 us  [on_device(): lax.psum_scatter(partial_x, 'row', scatter_dimension=1, tiled=True)]
    psum x1 -> x2, blocking collectives: 76.1 us -> 87.6 us  [the longest x1 57.7 us: on_device(): lax.psum(lax.psum((weight_term, bias_term), 'row'), 'col')]
  transfers between devices with their start and end apart: 5 -> 6, of which waited for: 5 -> 6; matrix products, arithmetic and copies ran while one was open for 15% -> 13% of each run, Pallas kernels for 0% -> 0%
where the time goes in v1:
time: 913 us; the launch traced here: 911 us
  waiting for transfers between devices  556 us (61%)
  other arithmetic  138 us (15%)
  blocking collectives  87.6 us (10%)
  matrix products  63.6 us (7%)
  local copies, waits for them, and re-layouts  51.4 us (6%)
  between operations  14.2 us (2%)
    reduce_scatter x1, waiting for transfers between devices, on_device(): lax.psum_scatter(partial_value, 'col', scatter_dimension=0, tiled=True)  139 us
    scatter-add x8, other arithmetic, one_group(): return totals.at[put_to].add(products)  128 us
    psum x1, waiting for transfers between devices, on_device(): lax.psum((weight_term, bias_term), 'row')  110 us
    reduce_scatter x1, waiting for transfers between devices, on_device(): lax.psum_scatter(partial_x, 'row', scatter_dimension=1, tiled=True)  109 us
    psum x1, waiting for transfers between devices, on_device(): lax.psum(lax.psum((weight_term, bias_term), 'row'), 'col')  69.7 us
    all_gather x1, waiting for transfers between devices, on_device(): feat_tile = lax.all_gather(features, 'row', axis=1, tiled=True)  66.8 us
    all_gather x1, waiting for transfers between devices, on_device(): grad_tile = lax.all_gather(grad_agg, 'col', axis=0, tiled=True)  60.3 us
    dot_general x8, matrix products, one_group(): jnp.einsum(pattern, slab_vals, picked, preferred_element_type=jnp.float32)  59 us
  transfers between devices with their start and end apart: 6, of which 6 were waited for; matrix products, arithmetic and copies ran while one was open for 13% of the time, Pallas kernels for 0%

profile of v1, /device:TPU:2, one launch (start us, length us, event | category | flops | bytes accessed | tf_op | source)
XLA Modules:
  0.0 911.4 jit_solution(9639546746695550001)
XLA Ops:
  8.7 66.8 %all-gather.3.cloned.1.call-done = bf16[2048,256]{0,1:T(8,128)(2,1)} async-done(((bf16[2048,32]{0,1:T(8,128)(2,1)}), bf16[2048,256]{0,1:T(8,128)(2,1)}) %all-gather.3.cloned.1.call-update) | async-done | bytes 1048592 | tf_op jit(solution)/shard_map/all_gather | solution.py:40
  81.3 122.1 %while.28 = (s32[]{:T(128)}, f32[64,128,256]{2,1,0:T(8,128)}, s32[256]{0:T(256)S(1)}, s32[]{:T(128)}, bf16[256,128,128]{2,1,0:T(8,128)(2,1)}, /*index=5*/s32[256...) while((s32[]{:T(128)}, f32[64,128,256]{2,1,0:T(8,128)}, ...), condition=%wide.region_2.3_spmd.clone, body=%wide.region_0.2_spmd.clone.sunk | while | flops 543164096 | bytes 48240816 | solution.py:29
  84.7 7.4 broadcast_select_fusion.4
  92.2 19.7 %scatter_fusion = f32[64,128,256]{2,1,0:T(8,128)} fusion(f32[64,128,256]{2,1,0:T(8,128)} %get-tuple-element.472, s32[64]{0:T(128)S(1)} %compare_select_fusion.8, f32[64,128,256]{2,1,0:T(8,128)} %broadcast_select_fusion.4), kind=kCustom, calls=%fused_computation.2.clone.clone.1 | custom fusion | flops 2097152 | bytes 25166080 | tf_op jit(solution)/shard_map/while/body/eval_jaxpr/scatter-add | solution.py:25
  115.4 7.4 broadcast_select_fusion.4
  122.8 19.6 %scatter_fusion = f32[64,128,256]{2,1,0:T(8,128)} fusion(f32[64,128,256]{2,1,0:T(8,128)} %get-tuple-element.472, s32[64]{0:T(128)S(1)} %compare_select_fusion.8, f32[64,128,256]{2,1,0:T(8,128)} %broadcast_select_fusion.4), kind=kCustom, calls=%fused_computation.2.clone.clone.1 | custom fusion | flops 2097152 | bytes 25166080 | tf_op jit(solution)/shard_map/while/body/eval_jaxpr/scatter-add | solution.py:25
  145.9 7.4 broadcast_select_fusion.4
  153.4 19.6 %scatter_fusion = f32[64,128,256]{2,1,0:T(8,128)} fusion(f32[64,128,256]{2,1,0:T(8,128)} %get-tuple-element.472, s32[64]{0:T(128)S(1)} %compare_select_fusion.8, f32[64,128,256]{2,1,0:T(8,128)} %broadcast_select_fusion.4), kind=kCustom, calls=%fused_computation.2.clone.clone.1 | custom fusion | flops 2097152 | bytes 25166080 | tf_op jit(solution)/shard_map/while/body/eval_jaxpr/scatter-add | solution.py:25
  183.9 19.5 %scatter_fusion = f32[64,128,256]{2,1,0:T(8,128)} fusion(f32[64,128,256]{2,1,0:T(8,128)} %get-tuple-element.472, s32[64]{0:T(128)S(1)} %compare_select_fusion.8, f32[64,128,256]{2,1,0:T(8,128)} %broadcast_select_fusion.4), kind=kCustom, calls=%fused_computation.2.clone.clone.1 | custom fusion | flops 2097152 | bytes 25166080 | tf_op jit(solution)/shard_map/while/body/eval_jaxpr/scatter-add | solution.py:25
  203.4 138.6 %reduce-scatter.3.cloned.1.call-done = f32[256,256]{1,0:T(8,128)} async-done(((f32[8192,256]{1,0:T(8,128)}), f32[256,256]{1,0:T(8,128)}) %reduce-scatter.3.cloned.1.call-update) | async-done | bytes 262160 | tf_op jit(solution)/shard_map/reduce_scatter | solution.py:48
  346.9 12.0 %copy.11 = bf16[1,1,256,128,128]{3,4,2,1,0:T(8,128)(2,1)} copy(bf16[1,1,256,128,128]{4,3,2,1,0:T(8,128)(2,1)} %bitcast.18) | data formatting | bytes 16777216 | tf_op args[1]
  358.8 110.1 %all-reduce.3.cloned.1.call-done = f32[256,256]{1,0:T(8,128)} async-done(((f32[256,256]{1,0:T(8,128)}), f32[256,256]{1,0:T(8,128)}) %all-reduce.3.cloned.1.call-update) | async-done | bytes 262160 | tf_op jit(solution)/shard_map/psum | solution.py:60
  469.0 60.3 %all-gather.5.cloned.1.call-done = bf16[8192,256]{1,0:T(8,128)(2,1)} async-done(((bf16[256,256]{1,0:T(8,128)(2,1)}), bf16[8192,256]{1,0:T(8,128)(2,1)}) %all-gather.5.cloned.1.call-update) | async-done | bytes 4194320 | tf_op jit(solution)/shard_map/all_gather | solution.py:67
  529.5 102.5 %while.29 = (s32[]{:T(128)}, f32[16,128,256]{2,1,0:T(8,128)S(1)}, s32[256]{0:T(256)S(1)}, s32[]{:T(128)}, bf16[256,128,128]{1,2,0:T(8,128)(2,1)}, /*index=5*/s32...) while((s32[]{:T(128)}, f32[16,128,256]{2,1,0:T(8,128)S(1)}, ...), condition=%wide.region_6.7_spmd.clone, body=%wide.region_4.6_spmd.clone.sunk | while | flops 543164096 | bytes 48240816 | solution.py:29
  542.7 12.4 %scatter_fusion.1 = f32[16,128,256]{2,1,0:T(8,128)S(1)} fusion(f32[16,128,256]{2,1,0:T(8,128)S(1)} %get-tuple-element.505, s32[64]{0:T(128)S(1)} %compare_select_fusion.9, f32[64,128,256]{2,1,0:T(8,128)} %broadcast_select_fusion.5), kind=kCustom, calls=%fused_computation.3.clone.clone.1 | custom fusion | flops 2097152 | bytes 25166080 | tf_op jit(solution)/shard_map/while/body/eval_jaxpr/scatter-add | solution.py:25
  560.9 7.4 broadcast_select_fusion.5
  568.3 12.5 %scatter_fusion.1 = f32[16,128,256]{2,1,0:T(8,128)S(1)} fusion(f32[16,128,256]{2,1,0:T(8,128)S(1)} %get-tuple-element.505, s32[64]{0:T(128)S(1)} %compare_select_fusion.9, f32[64,128,256]{2,1,0:T(8,128)} %broadcast_select_fusion.5), kind=kCustom, calls=%fused_computation.3.clone.clone.1 | custom fusion | flops 2097152 | bytes 25166080 | tf_op jit(solution)/shard_map/while/body/eval_jaxpr/scatter-add | solution.py:25
  594.0 12.4 %scatter_fusion.1 = f32[16,128,256]{2,1,0:T(8,128)S(1)} fusion(f32[16,128,256]{2,1,0:T(8,128)S(1)} %get-tuple-element.505, s32[64]{0:T(128)S(1)} %compare_select_fusion.9, f32[64,128,256]{2,1,0:T(8,128)} %broadcast_select_fusion.5), kind=kCustom, calls=%fused_computation.3.clone.clone.1 | custom fusion | flops 2097152 | bytes 25166080 | tf_op jit(solution)/shard_map/while/body/eval_jaxpr/scatter-add | solution.py:25
  612.2 7.4 broadcast_select_fusion.5
  619.6 12.4 %scatter_fusion.1 = f32[16,128,256]{2,1,0:T(8,128)S(1)} fusion(f32[16,128,256]{2,1,0:T(8,128)S(1)} %get-tuple-element.505, s32[64]{0:T(128)S(1)} %compare_select_fusion.9, f32[64,128,256]{2,1,0:T(8,128)} %broadcast_select_fusion.5), kind=kCustom, calls=%fused_computation.3.clone.clone.1 | custom fusion | flops 2097152 | bytes 25166080 | tf_op jit(solution)/shard_map/while/body/eval_jaxpr/scatter-add | solution.py:25
  634.0 30.0 %psum.30 = f32[256]{0:T(256)S(1)} all-reduce(f32[256]{0:T(256)S(1)} %get-tuple-element.355), channel_id=1, replica_groups=mesh['row'=8,'col'=32] {'row'}, use_global_device_ids=true, to_apply=%region_11.12 | all-reduce | flops 256 | bytes 2048 | tf_op jit(solution)/shard_map/psum | solution.py:60
  663.9 57.7 %psum.31 = f32[256]{0:T(256)S(1)} all-reduce(f32[256]{0:T(256)S(1)} %psum.30), channel_id=1, replica_groups=mesh['row'=8,'col'=32] {'col'}, use_global_device_ids=true, to_apply=%region_12.13 | all-reduce | flops 256 | bytes 2048 | tf_op jit(solution)/shard_map/psum | solution.py:60
  722.2 69.7 %all-reduce.5.cloned.1.call-done = f32[256,256]{1,0:T(8,128)} async-done(((f32[256,256]{1,0:T(8,128)}), f32[256,256]{1,0:T(8,128)}) %all-reduce.5.cloned.1.call-update) | async-done | bytes 262160 | tf_op jit(solution)/shard_map/psum | solution.py:60
  793.6 109.4 %reduce-scatter.5.cloned.1.call-done = f32[2048,32]{0,1:T(8,128)} async-done(((f32[2048,256]{0,1:T(8,128)}), f32[2048,32]{0,1:T(8,128)}) %reduce-scatter.5.cloned.1.call-update) | async-done | bytes 262160 | tf_op jit(solution)/shard_map/reduce_scatter | solution.py:73
  (64 shorter events, 77.5 us)
Async XLA Ops:
  7.2 334.9 %copy-start = (bf16[256,256]{1,0:T(8,128)(2,1)S(1)}, bf16[256,256]{1,0:T(8,128)(2,1)}, u32[]{:S(2)}) copy-start(bf16[256,256]{1,0:T(8,128)(2,1)} %param.15) | copy-start | bytes 393220
  7.2 68.4 %all-gather.3.cloned.1.call-start = ((), (), s32[]{:S(2)}) async-start(), calls=%async_computation.2 | async-start | bytes 1179648 | tf_op jit(solution)/shard_map/all_gather | solution.py:40
  7.9 334.1 %reduce-scatter.3.cloned.1.call-start = ((), (), s32[]{:S(2)}) async-start(), calls=%async_computation.3 | async-start | bytes 8650752 | tf_op jit(solution)/shard_map/reduce_scatter | solution.py:48
  203.4 138.7 %copy-start.1 = (bf16[256,256]{1,0:T(8,128)(2,1)S(1)}, bf16[256,256]{1,0:T(8,128)(2,1)}, u32[]{:S(2)}) copy-start(bf16[256,256]{1,0:T(8,128)(2,1)} %param.17) | copy-start | bytes 393220
  203.4 138.7 %copy-start.2 = (f32[256]{0:T(256)S(1)}, f32[256]{0:T(256)}, u32[]{:S(2)}) copy-start(f32[256]{0:T(256)} %param.16) | copy-start | bytes 3076
  203.4 265.5 %all-reduce.3.cloned.1.call-start = ((), (), s32[]{:S(2)}) async-start(), calls=%async_computation.6 | async-start | bytes 524288 | tf_op jit(solution)/shard_map/psum | solution.py:60
  345.9 183.5 %all-gather.5.cloned.1.call-start = ((), (), s32[]{:S(2)}) async-start(), calls=%async_computation.4 | async-start | bytes 4325376 | tf_op jit(solution)/shard_map/all_gather | solution.py:67
  346.8 445.1 %all-reduce.5.cloned.1.call-start = ((), (), s32[]{:S(2)}) async-start(), calls=%async_computation.7 | async-start | bytes 524288 | tf_op jit(solution)/shard_map/psum | solution.py:60
  469.0 434.0 %reduce-scatter.5.cloned.1.call-start = ((), (), s32[]{:S(2)}) async-start(), calls=%async_computation.5 | async-start | bytes 2359296 | tf_op jit(solution)/shard_map/reduce_scatter | solution.py:73
Sparse Core Ops, SparseCore 0:
  10.6 64.8 all-gather.2
  203.5 138.4 reduce-scatter.2
  346.0 122.9 all-reduce.2
  471.4 57.8 all-gather.4
  532.0 259.9 all-reduce.4
  795.8 107.0 reduce-scatter.4
